TPU v7x, 32 devices: a whole 2x2x4 slice. The times are simulated.
32 devices in a mesh: dp: 2 (over x), wide: 4 (over z), narrow: 4 (over y, core).
Axes of the slice: x: 2, y: 2, z: 4, core: 2. Of those that a mesh axis runs over, the one named last changes fastest.
Arguments:
- tokens: bfloat16 [8192, 2048], P(('dp', 'wide'), 'narrow'), may hold values from -6 to 6
- continuation_lengths: int32 [2, 8], P('dp'), may hold values from 1 to 511, 2048 in all within a row
- attention_gain: float32 [2048], replicated, may hold values from 0.5 to 1.5
- query_weight: bfloat16 [2048, 2048], P('narrow', 'wide'), may hold values from -0.125 to 0.125
- key_weight: bfloat16 [2048, 1024], P('narrow', 'wide'), may hold values from -0.125 to 0.125
- value_weight: bfloat16 [2048, 1024], P('narrow', 'wide'), may hold values from -0.125 to 0.125
- head_gate: bfloat16 [2048, 16], P('narrow', 'wide'), may hold values from -0.125 to 0.125
- query_gain: float32 [128], replicated, may hold values from 0.5 to 1.5
- key_gain: float32 [128], replicated, may hold values from 0.5 to 1.5
- output_weight: bfloat16 [2048, 2048], P('wide', 'narrow'), may hold values from -2 to 2
- feedforward_gain: float32 [2048], replicated, may hold values from 0.5 to 1.5
- gate_weight: bfloat16 [2048, 6144], P('narrow', 'wide'), may hold values from -0.125 to 0.125
- up_weight: bfloat16 [2048, 6144], P('narrow', 'wide'), may hold values from -0.125 to 0.125
- down_weight: bfloat16 [6144, 2048], P('wide', 'narrow'), may hold values from -0.078125 to 0.078125
- cotangent: bfloat16 [8192, 2048], P(('dp', 'wide'), 'narrow'), may hold values from -6 to 6
Outputs:
- layer_output: bfloat16 [8192, 2048], P(('dp', 'wide'), 'narrow')
- tokens_gradient: float32 [8192, 2048], P(('dp', 'wide'), 'narrow')
- attention_gain_gradient: float32 [2048], replicated
- query_gradient: float32 [2048, 2048], P('narrow', 'wide')
- key_gradient: float32 [2048, 1024], P('narrow', 'wide')
- value_gradient: float32 [2048, 1024], P('narrow', 'wide')
- head_gate_gradient: float32 [2048, 16], P('narrow', 'wide')
- query_gain_gradient: float32 [128], replicated
- key_gain_gradient: float32 [128], replicated
- output_gradient: float32 [2048, 2048], P('wide', 'narrow')
- feedforward_gain_gradient: float32 [2048], replicated
- gate_gradient: float32 [2048, 6144], P('narrow', 'wide')
- up_gradient: float32 [2048, 6144], P('narrow', 'wide')
- down_gradient: float32 [6144, 2048], P('wide', 'narrow')
Inputs may be any that keep to these rules, and one draw needn't show every extreme that they name: `continuation_lengths`: each group's 8 lengths sum to 2048, and one of them is exactly 511.
All inputs are finite; a program needn't handle non-finite values.
Results may differ from a plain program's by a relative error of at most 0.018.
Values may be sent and summed in bfloat16 or wider, within the bound.
A program may use at most 320 MiB of HBM per device.

v0:
```python
import jax
import jax.numpy as jnp
from jax import lax
from jax.sharding import PartitionSpec as P

PROMPT = 2048
EPS = 1e-06
THETA = 1000000.0


def dot_rows(left, right):
    return jnp.dot(left, right, preferred_element_type=jnp.float32)


def dot_trans(left, right):
    return lax.dot_general(
        left, right, (((1,), (1,)), ((), ())), preferred_element_type=jnp.float32
    )


def dot_inner(left, right):
    return lax.dot_general(
        left, right, (((0,), (0,)), ((), ())), preferred_element_type=jnp.float32
    )


def expand(local_rows, weight, transpose):
    gathered = lax.all_gather(local_rows, "wide", axis=0, tiled=True)

    def expand_partial_term():
        if transpose:
            return dot_trans(gathered, weight)
        return dot_rows(gathered, weight)

    return (
        gathered,
        lax.psum_scatter(expand_partial_term(), "narrow", scatter_dimension=0, tiled=True),
    )


def contract(local_rows, weight, transpose):
    gathered = lax.all_gather(local_rows, "narrow", axis=0, tiled=True)

    def contract_partial_term():
        if transpose:
            return dot_trans(gathered, weight)
        return dot_rows(gathered, weight)

    return (
        gathered,
        lax.psum_scatter(contract_partial_term(), "wide", scatter_dimension=0, tiled=True),
    )


def row_total(values):
    return lax.psum(values, "narrow")


def layout(lengths, group_rows):
    ends = jnp.cumsum(lengths)
    starts = ends - lengths
    index = jnp.arange(group_rows, dtype=jnp.int32)
    offset = index - PROMPT
    member = ((offset[:, None] >= starts[None, :]) & (offset[:, None] < ends[None, :])).astype(
        jnp.int32
    )
    numbers = jnp.arange(1, lengths.shape[0] + 1, dtype=jnp.int32)
    segment = jnp.sum(member * numbers[None, :], axis=1)
    position = index - jnp.sum(member * starts[None, :], axis=1)
    return (index, segment, position)


def rope_tables(position, head_size):
    frequency = THETA ** (-2.0 * jnp.arange(head_size // 2, dtype=jnp.float32) / head_size)
    angle = position.astype(jnp.float32)[:, None] * frequency[None, :]
    return (jnp.cos(angle)[:, None, :], jnp.sin(angle)[:, None, :])


def rotate(values, cosine, sine):
    half = values.shape[-1] // 2
    first = values[..., :half]
    second = values[..., half:]
    return jnp.concatenate(
        [first * cosine - second * sine, second * cosine + first * sine], axis=-1
    )


def rotate_back(upstream, cosine, sine):
    half = upstream.shape[-1] // 2
    first = upstream[..., :half]
    second = upstream[..., half:]
    return jnp.concatenate(
        [first * cosine + second * sine, second * cosine - first * sine], axis=-1
    )


def head_norm(raw, gain):
    inverse = lax.rsqrt(jnp.mean(raw * raw, axis=-1, keepdims=True) + EPS)
    normal = raw * inverse
    return (normal, inverse, normal * gain)


def head_norm_back(upstream, normal, inverse, gain):
    scaled = upstream * gain
    gain_term = jnp.sum(upstream * normal, axis=(0, 1))
    inner = jnp.mean(scaled * normal, axis=-1, keepdims=True)
    return (inverse * (scaled - normal * inner), gain_term)


def visible(row_index, row_segment, index, segment):
    return (index[None, :] <= row_index[:, None]) & (
        (segment[None, :] == 0) | (segment[None, :] == row_segment[:, None])
    )


def block_scores(grouped, keys_all, allowed, scale):
    scores = (
        jnp.einsum("bkrd,tkd->krbt", grouped, keys_all, preferred_element_type=jnp.float32) * scale
    )
    return jnp.where(allowed[None, None], scores, -1e30)


def on_device(
    tokens,
    continuation_lengths,
    attention_gain,
    query_weight,
    key_weight,
    value_weight,
    head_gate,
    query_gain,
    key_gain,
    output_weight,
    feedforward_gain,
    gate_weight,
    up_weight,
    down_weight,
    cotangent,
):
    rows_wide, width_local = tokens.shape
    width_full = attention_gain.shape[0]
    head_size = query_gain.shape[0]
    heads_local = head_gate.shape[1]
    pair_heads = key_weight.shape[1] // head_size
    hidden_local = gate_weight.shape[1]
    group_rows = rows_wide * lax.axis_size("wide")
    rows_narrow = group_rows // lax.axis_size("narrow")
    narrow_index = lax.axis_index("narrow")
    repeat = heads_local // pair_heads
    block = 512
    blocks = rows_narrow // block
    scale = head_size ** (-0.5)
    query_cols = heads_local * head_size
    key_cols = pair_heads * head_size
    index, segment, position = layout(continuation_lengths[0], group_rows)
    my_start = narrow_index * rows_narrow
    my_index = lax.dynamic_slice_in_dim(index, my_start, rows_narrow)
    my_segment = lax.dynamic_slice_in_dim(segment, my_start, rows_narrow)
    my_position = lax.dynamic_slice_in_dim(position, my_start, rows_narrow)
    cosine, sine = rope_tables(my_position, head_size)
    gain_one = lax.dynamic_slice_in_dim(attention_gain, narrow_index * width_local, width_local)
    gain_two = lax.dynamic_slice_in_dim(feedforward_gain, narrow_index * width_local, width_local)
    inputs = tokens.astype(jnp.float32)
    inverse_one = lax.rsqrt(row_total(jnp.sum(inputs * inputs, axis=1)) / width_full + EPS)[:, None]
    hat_one = inputs * inverse_one
    normed = (hat_one * gain_one).astype(jnp.bfloat16)
    joined_weight = jnp.concatenate([query_weight, key_weight, value_weight, head_gate], axis=1)
    normed_all, projected = expand(normed, joined_weight, False)
    query_raw = projected[:, :query_cols].reshape(rows_narrow, heads_local, head_size)
    key_raw = projected[:, query_cols : query_cols + key_cols].reshape(
        rows_narrow, pair_heads, head_size
    )
    value_raw = projected[:, query_cols + key_cols : query_cols + 2 * key_cols]
    gate_logit = projected[:, query_cols + 2 * key_cols :]
    query_hat, query_inverse, query_normed = head_norm(query_raw, query_gain)
    key_hat, key_inverse, key_normed = head_norm(key_raw, key_gain)
    queries = rotate(query_normed, cosine, sine).astype(jnp.bfloat16)
    keys_local = rotate(key_normed, cosine, sine).astype(jnp.bfloat16)
    values_local = value_raw.reshape(rows_narrow, pair_heads, head_size).astype(jnp.bfloat16)
    keys_all, values_all = (
        lax.all_gather(keys_local, "narrow", axis=0, tiled=True),
        lax.all_gather(values_local, "narrow", axis=0, tiled=True),
    )

    def attend(block_inputs):
        query_block, row_index, row_segment = block_inputs
        grouped = query_block.reshape(block, pair_heads, repeat, head_size)
        scores = block_scores(
            grouped, keys_all, visible(row_index, row_segment, index, segment), scale
        )
        peak = jnp.max(scores, axis=-1, keepdims=True)
        weights = jnp.exp(scores - peak)
        total = jnp.sum(weights, axis=-1, keepdims=True)
        probs = weights / total
        context_block = jnp.einsum(
            "krbt,tkd->bkrd",
            probs.astype(jnp.bfloat16),
            values_all,
            preferred_element_type=jnp.float32,
        )
        return (
            context_block.reshape(block, heads_local, head_size),
            (peak + jnp.log(total))[..., 0],
        )

    query_blocks = queries.reshape(blocks, block, heads_local, head_size)
    index_blocks = my_index.reshape(blocks, block)
    segment_blocks = my_segment.reshape(blocks, block)
    context, log_total = lax.map(attend, (query_blocks, index_blocks, segment_blocks))
    context = context.reshape(rows_narrow, heads_local, head_size)
    gate = jax.nn.sigmoid(gate_logit)
    gated = (context * gate[:, :, None]).astype(jnp.bfloat16).reshape(rows_narrow, query_cols)
    context_all, attention_term = contract(gated, output_weight, False)
    middle = inputs + attention_term
    inverse_two = lax.rsqrt(row_total(jnp.sum(middle * middle, axis=1)) / width_full + EPS)[:, None]
    hat_two = middle * inverse_two
    normed_two = (hat_two * gain_two).astype(jnp.bfloat16)
    gate_up_weight = jnp.concatenate([gate_weight, up_weight], axis=1)
    normed_two_all, gate_up = expand(normed_two, gate_up_weight, False)
    gate_pre = gate_up[:, :hidden_local]
    up_pre = gate_up[:, hidden_local:]
    hidden = (jax.nn.silu(gate_pre) * up_pre).astype(jnp.bfloat16)
    hidden_all, mlp_term = contract(hidden, down_weight, False)
    layer_output = (middle + mlp_term).astype(jnp.bfloat16)
    upstream_all, hidden_grad = expand(cotangent, down_weight, True)
    down_grad = dot_inner(hidden_all, upstream_all)
    gate_sigmoid = jax.nn.sigmoid(gate_pre)
    gate_grad = hidden_grad * up_pre * gate_sigmoid * (1.0 + gate_pre * (1.0 - gate_sigmoid))
    up_grad = hidden_grad * jax.nn.silu(gate_pre)
    gate_up_low = jnp.concatenate([gate_grad, up_grad], axis=1).astype(jnp.bfloat16)
    gate_up_all, normed_two_grad = contract(gate_up_low, gate_up_weight, True)
    gate_up_grad = dot_inner(normed_two_all, gate_up_all)
    gain_two_term = jnp.sum(normed_two_grad * hat_two, axis=0)
    scaled_two = normed_two_grad * gain_two
    inner_two = row_total(jnp.sum(scaled_two * hat_two, axis=1))[:, None] / width_full
    middle_grad = cotangent.astype(jnp.float32) + inverse_two * (scaled_two - hat_two * inner_two)
    middle_low = middle_grad.astype(jnp.bfloat16)
    middle_all, gated_grad = expand(middle_low, output_weight, True)
    output_grad = dot_inner(context_all, middle_all)
    gated_grad = gated_grad.reshape(rows_narrow, heads_local, head_size)
    context_grad = (gated_grad * gate[:, :, None]).astype(jnp.bfloat16)
    gate_logit_grad = jnp.sum(gated_grad * context, axis=2) * gate * (1.0 - gate)

    def attend_back(carry, block_inputs):
        key_sum, value_sum = carry
        query_block, grad_block, log_block, row_index, row_segment = block_inputs
        grouped = query_block.reshape(block, pair_heads, repeat, head_size)
        grad_grouped = grad_block.reshape(block, pair_heads, repeat, head_size)
        scores = block_scores(
            grouped, keys_all, visible(row_index, row_segment, index, segment), scale
        )
        probs = jnp.exp(scores - log_block[..., None])
        prob_grads = jnp.einsum(
            "bkrd,tkd->krbt", grad_grouped, values_all, preferred_element_type=jnp.float32
        )
        inner = jnp.sum(probs * prob_grads, axis=-1, keepdims=True)
        score_grads = (probs * (prob_grads - inner)).astype(jnp.bfloat16)
        query_part = (
            jnp.einsum("krbt,tkd->bkrd", score_grads, keys_all, preferred_element_type=jnp.float32)
            * scale
        )
        key_sum = (
            key_sum
            + jnp.einsum("krbt,bkrd->tkd", score_grads, grouped, preferred_element_type=jnp.float32)
            * scale
        )
        value_sum = value_sum + jnp.einsum(
            "krbt,bkrd->tkd",
            probs.astype(jnp.bfloat16),
            grad_grouped,
            preferred_element_type=jnp.float32,
        )
        return ((key_sum, value_sum), query_part.reshape(block, heads_local, head_size))

    empty = jnp.zeros((group_rows, pair_heads, head_size), jnp.float32)
    grad_blocks = context_grad.reshape(blocks, block, heads_local, head_size)
    (key_sum, value_sum), query_grads = lax.scan(
        attend_back,
        (empty, empty),
        (query_blocks, grad_blocks, log_total, index_blocks, segment_blocks),
    )
    query_grads = query_grads.reshape(rows_narrow, heads_local, head_size)
    key_mine, value_mine = (
        lax.psum_scatter(
            key_sum.astype(jnp.bfloat16), "narrow", scatter_dimension=0, tiled=True
        ).astype(jnp.float32),
        lax.psum_scatter(
            value_sum.astype(jnp.bfloat16), "narrow", scatter_dimension=0, tiled=True
        ).astype(jnp.float32),
    )
    query_raw_grad, query_gain_term = head_norm_back(
        rotate_back(query_grads, cosine, sine), query_hat, query_inverse, query_gain
    )
    key_raw_grad, key_gain_term = head_norm_back(
        rotate_back(key_mine, cosine, sine), key_hat, key_inverse, key_gain
    )
    joined_low = jnp.concatenate(
        [
            query_raw_grad.reshape(rows_narrow, query_cols),
            key_raw_grad.reshape(rows_narrow, key_cols),
            value_mine.reshape(rows_narrow, key_cols),
            gate_logit_grad,
        ],
        axis=1,
    ).astype(jnp.bfloat16)
    joined_all, normed_grad = contract(joined_low, joined_weight, True)
    joined_grad = dot_inner(normed_all, joined_all)
    gain_one_term = jnp.sum(normed_grad * hat_one, axis=0)
    scaled_one = normed_grad * gain_one
    inner_one = row_total(jnp.sum(scaled_one * hat_one, axis=1))[:, None] / width_full
    tokens_gradient = middle_grad + inverse_one * (scaled_one - hat_one * inner_one)
    joined_grad, output_grad, gate_up_grad, down_grad = (
        lax.psum(joined_grad.astype(jnp.bfloat16), "dp").astype(jnp.float32),
        lax.psum(output_grad.astype(jnp.bfloat16), "dp").astype(jnp.float32),
        lax.psum(gate_up_grad.astype(jnp.bfloat16), "dp").astype(jnp.float32),
        lax.psum(down_grad.astype(jnp.bfloat16), "dp").astype(jnp.float32),
    )
    gain_one_full = lax.dynamic_update_slice_in_dim(
        jnp.zeros_like(attention_gain), gain_one_term, narrow_index * width_local, 0
    )
    gain_two_full = lax.dynamic_update_slice_in_dim(
        jnp.zeros_like(feedforward_gain), gain_two_term, narrow_index * width_local, 0
    )
    gain_one_full, gain_two_full, query_gain_term, key_gain_term = lax.psum(
        (gain_one_full, gain_two_full, query_gain_term, key_gain_term), ("dp", "wide", "narrow")
    )
    query_gradient = joined_grad[:, :query_cols]
    key_gradient = joined_grad[:, query_cols : query_cols + key_cols]
    value_gradient = joined_grad[:, query_cols + key_cols : query_cols + 2 * key_cols]
    head_gate_gradient = joined_grad[:, query_cols + 2 * key_cols :]
    gate_gradient = gate_up_grad[:, :hidden_local]
    up_gradient = gate_up_grad[:, hidden_local:]
    return (
        layer_output,
        tokens_gradient,
        gain_one_full,
        query_gradient,
        key_gradient,
        value_gradient,
        head_gate_gradient,
        query_gain_term,
        key_gain_term,
        output_grad,
        gain_two_full,
        gate_gradient,
        up_gradient,
        down_grad,
    )


def solution(mesh):
    return jax.shard_map(
        on_device,
        mesh=mesh,
        in_specs=(
            P(("dp", "wide"), "narrow"),
            P("dp", None),
            P(),
            P("narrow", "wide"),
            P("narrow", "wide"),
            P("narrow", "wide"),
            P("narrow", "wide"),
            P(),
            P(),
            P("wide", "narrow"),
            P(),
            P("narrow", "wide"),
            P("narrow", "wide"),
            P("wide", "narrow"),
            P(("dp", "wide"), "narrow"),
        ),
        out_specs=(
            P(("dp", "wide"), "narrow"),
            P(("dp", "wide"), "narrow"),
            P(),
            P("narrow", "wide"),
            P("narrow", "wide"),
            P("narrow", "wide"),
            P("narrow", "wide"),
            P(),
            P(),
            P("wide", "narrow"),
            P(),
            P("narrow", "wide"),
            P("narrow", "wide"),
            P("wide", "narrow"),
        ),
        check_vma=False,
    )
```

profile of v0, /device:TPU:0, one launch (start us, length us, event | category | flops | bytes accessed | tf_op | source)
XLA Modules:
  0.0 2702.8 jit_solution(11104213106023687378)
XLA Ops:
  21.5 80.9 %all-gather.11.cloned.1.call-done = bf16[4096,512]{1,0:T(8,128)(2,1)} async-done(((bf16[1024,512]{1,0:T(8,128)(2,1)}), bf16[4096,512]{1,0:T(8,128)(2,1)}) %all-gather.11.cloned.1.call-update) | async-done | bytes 4194320 | tf_op jit(solution)/shard_map/all_gather | solution.py:28
  117.1 122.4 %reduce-scatter.11.cloned.1.call-done = f32[1024,1028]{0,1:T(8,128)} async-done(((f32[4096,1028]{0,1:T(8,128)}), f32[1024,1028]{0,1:T(8,128)}) %reduce-scatter.11.cloned.1.call-update) | async-done | bytes 4210704 | tf_op jit(solution)/shard_map/reduce_scatter | solution.py:37
  290.6 100.4 %while.28 = (s32[]{:T(128)}, f32[2,512,4,128]{3,1,2,0:T(8,128)}, f32[2,2,2,512]{3,2,1,0:T(2,128)S(1)}, s32[2,512]{1,0:T(2,128)S(1)}, s32[4096]{0:T(1024)S(1)}, /...) while((s32[]{:T(128)}, f32[2,512,4,128]{3,1,2,0:T(8,128)}, ...), condition=%wide.region_11.12_spmd.clone, body=%wide.region_8.11_spmd.clone.sunk | while | flops 4404021248 | bytes 134860992 | solution.py:209
  397.0 34.2 %all-gather.17.cloned.1.call-done = bf16[4096,512]{1,0:T(8,128)(2,1)} async-done(((bf16[1024,512]{1,0:T(8,128)(2,1)}), bf16[4096,512]{1,0:T(8,128)(2,1)}) %all-gather.17.cloned.1.call-update) | async-done | bytes 4194320 | tf_op jit(solution)/shard_map/all_gather | solution.py:42
  440.6 143.2 %reduce-scatter.13.cloned.1.call-done = f32[1024,512]{1,0:T(8,128)} async-done(((f32[4096,512]{1,0:T(8,128)}), f32[1024,512]{1,0:T(8,128)}) %reduce-scatter.13.cloned.1.call-update) | async-done | bytes 2097168 | tf_op jit(solution)/shard_map/reduce_scatter | solution.py:51
  596.3 70.5 %all-gather.23.cloned.1.call-done = bf16[4096,512]{1,0:T(8,128)(2,1)} async-done(((bf16[1024,512]{1,0:T(8,128)(2,1)}), bf16[4096,512]{1,0:T(8,128)(2,1)}) %all-gather.23.cloned.1.call-update) | async-done | bytes 4194320 | tf_op jit(solution)/shard_map/all_gather | solution.py:28
  685.5 62.6 %all-gather.19.cloned.1.call-done = bf16[4096,512]{1,0:T(8,128)(2,1)} async-done(((bf16[1024,512]{1,0:T(8,128)(2,1)}), bf16[4096,512]{1,0:T(8,128)(2,1)}) %all-gather.19.cloned.1.call-update) | async-done | bytes 4194320 | tf_op jit(solution)/shard_map/all_gather | solution.py:28
  748.1 36.5 %fusion.76 = f32[4096,3072]{1,0:T(8,128)} fusion(bf16[4096,512]{1,0:T(8,128)(2,1)} %all-gather.19.cloned.1.call-done, bf16[512,3072]{1,0:T(8,128)(2,1)} %constant_dynamic-update-slice_fusion.2), kind=kOutput, calls=%fused_computation.169 | convolution fusion | flops 12884901888 | bytes 57671680 | tf_op jit(solution)/shard_map/dot_general | solution.py:12
  784.9 146.3 %reduce-scatter.19.cloned.1.call-done = f32[1024,1536]{1,0:T(8,128)} async-done(((f32[4096,1536]{1,0:T(8,128)}), f32[1024,1536]{1,0:T(8,128)}) %reduce-scatter.19.cloned.1.call-update) | async-done | bytes 6291472 | tf_op jit(solution)/shard_map/reduce_scatter | solution.py:37
  931.2 349.0 %reduce-scatter.15.cloned.1.call-done = f32[1024,3072]{1,0:T(8,128)} async-done(((f32[4096,3072]{1,0:T(8,128)}), f32[1024,3072]{1,0:T(8,128)}) %reduce-scatter.15.cloned.1.call-update) | async-done | bytes 12582928 | tf_op jit(solution)/shard_map/reduce_scatter | solution.py:37
  1293.5 154.9 %all-gather.25.cloned.1.call-done = bf16[4096,3072]{1,0:T(8,128)(2,1)} async-done(((bf16[1024,3072]{1,0:T(8,128)(2,1)}), bf16[4096,3072]{1,0:T(8,128)(2,1)}) %all-gather.25.cloned.1.call-update) | async-done | bytes 25165840 | tf_op jit(solution)/shard_map/all_gather | solution.py:42
  1469.4 144.7 %reduce-scatter.21.cloned.1.call-done = f32[1024,512]{1,0:T(8,128)} async-done(((f32[4096,512]{1,0:T(8,128)}), f32[1024,512]{1,0:T(8,128)}) %reduce-scatter.21.cloned.1.call-update) | async-done | bytes 2097168 | tf_op jit(solution)/shard_map/reduce_scatter | solution.py:51
  1628.2 81.2 %all-gather.27.cloned.1.call-done = bf16[4096,512]{1,0:T(8,128)(2,1)} async-done(((bf16[1024,512]{1,0:T(8,128)(2,1)}), bf16[4096,512]{1,0:T(8,128)(2,1)}) %all-gather.27.cloned.1.call-update) | async-done | bytes 4194320 | tf_op jit(solution)/shard_map/all_gather | solution.py:28
  1717.3 70.0 %reduce-scatter.23.cloned.1.call-done = f32[1024,512]{1,0:T(8,128)} async-done(((f32[4096,512]{1,0:T(8,128)}), f32[1024,512]{1,0:T(8,128)}) %reduce-scatter.23.cloned.1.call-update) | async-done | bytes 2097168 | tf_op jit(solution)/shard_map/reduce_scatter | solution.py:37
  1793.1 223.9 %while.29 = (s32[]{:T(128)}, f32[4096,2,128]{0,2,1:T(8,128)}, f32[4096,2,128]{0,2,1:T(8,128)}, f32[2,512,4,128]{3,1,0,2:T(8,128)}, bf16[2,512,4,128]{3,1,2,0:T(8...) while((s32[]{:T(128)}, f32[4096,2,128]{0,2,1:T(8,128)}, ...), condition=%wide.region_24.25_spmd.clone, body=%wide.region_22.24_spmd.clone.sunk | while | flops 10877143040 | bytes 349286720 | solution.py:277
  1829.2 25.2 fusion.148
  1854.3 28.4 %fusion.149 = bf16[2,2,512,4096]{3,2,1,0:T(8,128)(2,1)} fusion(f32[2,512,2,4096]{3,1,2,0:T(8,128)} %get-tuple-element.583, f32[2,512,2,4096]{3,1,2,0:T(8,128)} %fusion.146, f32[2,2,512]{2,1,0:T(2,128)S(1)} %get-tuple-element.584, f32[2,2,512]{2,1,0:T(2,128)S(1)} %dynamic-slice_bitcast_fusion.2, pred[512,4096]{1,0:T(8,128)(4,1)} %fusion.147), kind=kLoop, calls=%fused_computation.26.clone.1 | loop fusion | flops 50331648 | bytes 85999616 | tf_op jit(solution)/shard_map/while/body/eval_jaxpr/convert_element_type | solution.py:257
  1966.6 28.4 %fusion.149 = bf16[2,2,512,4096]{3,2,1,0:T(8,128)(2,1)} fusion(f32[2,512,2,4096]{3,1,2,0:T(8,128)} %get-tuple-element.583, f32[2,512,2,4096]{3,1,2,0:T(8,128)} %fusion.146, f32[2,2,512]{2,1,0:T(2,128)S(1)} %get-tuple-element.584, f32[2,2,512]{2,1,0:T(2,128)S(1)} %dynamic-slice_bitcast_fusion.2, pred[512,4096]{1,0:T(8,128)(4,1)} %fusion.147), kind=kLoop, calls=%fused_computation.26.clone.1 | loop fusion | flops 50331648 | bytes 85999616 | tf_op jit(solution)/shard_map/while/body/eval_jaxpr/convert_element_type | solution.py:257
  2056.6 29.1 %reduce-scatter.27.cloned.1.call-done = bf16[1024,2,128]{0,2,1:T(8,128)(2,1)} async-done(((bf16[4096,2,128]{0,2,1:T(8,128)(2,1)}), bf16[1024,2,128]{0,2,1:T(8,128)(2,1)}) %reduce-scatter.27.cloned.1.call-update) | async-done | bytes 524304 | tf_op jit(solution)/shard_map/reduce_scatter | solution.py:287
  2088.3 81.5 %all-gather.21.cloned.1.call-done = bf16[4096,1536]{1,0:T(8,128)(2,1)} async-done(((bf16[1024,1536]{1,0:T(8,128)(2,1)}), bf16[4096,1536]{1,0:T(8,128)(2,1)}) %all-gather.21.cloned.1.call-update) | async-done | bytes 12582928 | tf_op jit(solution)/shard_map/all_gather | solution.py:42
  2266.7 127.6 %all-reduce.4.cloned.1.call-done = (bf16[512,1028]{0,1:T(8,128)(2,1)}, bf16[512,3072]{1,0:T(8,128)(2,1)}, bf16[512,512]{1,0:T(8,128)(2,1)}, bf16[1536,512]{1,0:T(8,128)(2,1)}) async-done(((bf16[512,1028]{0,1:T(8,128)(2,1)}, bf16[512,3072]{1,0:T(8,128)(2,1)}, bf16[512,512]{1,0:T(8,128)(2,1)}, bf16[1536,512]{1,0:T(8,128)(2,1)}), (bf16[512,1028]{0,1:T(8,128)(2,1)}, bf16[512,3072]{1,0:T(8,128)(2,1)}, ...) | async-done | bytes 6295568 | tf_op jit(solution)/shard_map/psum | solution.py:313
  2410.7 131.0 %reduce-scatter.29.cloned.1.call-done = f32[1024,512]{1,0:T(8,128)} async-done(((f32[4096,512]{1,0:T(8,128)}), f32[1024,512]{1,0:T(8,128)}) %reduce-scatter.29.cloned.1.call-update) | async-done | bytes 2097168 | tf_op jit(solution)/shard_map/reduce_scatter | solution.py:51
  2544.3 46.1 %all-reduce = (f32[2048]{0:T(1024)}, f32[128]{0:T(128)}, f32[128]{0:T(128)}, f32[2048]{0:T(1024)}) all-reduce(f32[2048]{0:T(1024)S(1)} %dynamic_update_slice.17, f32[128]{0:T(128)S(1)} %bitcast_reduce_fusion.1, f32[128]{0:T(128)S(1)} %bitcast_reduce_fusion.2, ...), channel_id=1, replica_groups=mesh['dp'=2,'wide'=4,'narrow'=4] {'dp','wide','narrow'}, use_global_device_ids=true, to_apply=%region_34.35 | all-reduce | flops 4352 | bytes 34816 | tf_op jit(solution)/shard_map/psum | solution.py:324
  2596.6 93.6 %reduce-scatter.17.cloned.1.call-done = f32[1024,512]{1,0:T(8,128)} async-done(((f32[4096,512]{1,0:T(8,128)}), f32[1024,512]{1,0:T(8,128)}) %reduce-scatter.17.cloned.1.call-update) | async-done | bytes 2097168 | tf_op jit(solution)/shard_map/reduce_scatter | solution.py:51
  (338 shorter events, 599.5 us)
Async XLA Ops:
  7.2 659.6 %copy-start = (bf16[1536,512]{1,0:T(8,128)(2,1)S(1)}, bf16[1536,512]{1,0:T(8,128)(2,1)}, u32[]{:S(2)}) copy-start(bf16[1536,512]{1,0:T(8,128)(2,1)} %param.32) | copy-start | bytes 4718596
  7.2 95.2 %all-gather.11.cloned.1.call-start = ((), (), s32[]{:S(2)}) async-start(), calls=%async_computation.10 | async-start | bytes 5242880 | tf_op jit(solution)/shard_map/all_gather | solution.py:28
  21.2 218.3 %reduce-scatter.11.cloned.1.call-start = ((), (), s32[]{:S(2)}) async-start(), calls=%async_computation.11 | async-start | bytes 21135360 | tf_op jit(solution)/shard_map/reduce_scatter | solution.py:37
  115.0 152.9 %all-gather.13.cloned.1.call-start = ((), (), s32[]{:S(2)}) async-start(), calls=%async_computation.12 | async-start | bytes 2621440 | tf_op jit(solution)/shard_map/all_gather | solution.py:181
  243.3 47.3 %all-gather.15.cloned.1.call-start = ((), (), s32[]{:S(2)}) async-start(), calls=%async_computation.13 | async-start | bytes 2621440 | tf_op jit(solution)/shard_map/all_gather | solution.py:182
  245.7 185.5 %all-gather.17.cloned.1.call-start = ((), (), s32[]{:S(2)}) async-start(), calls=%async_computation.14 | async-start | bytes 5242880 | tf_op jit(solution)/shard_map/all_gather | solution.py:42
  396.6 187.2 %reduce-scatter.13.cloned.1.call-start = ((), (), s32[]{:S(2)}) async-start(), calls=%async_computation.15 | async-start | bytes 10485760 | tf_op jit(solution)/shard_map/reduce_scatter | solution.py:51
  439.0 227.7 %all-gather.23.cloned.1.call-start = ((), (), s32[]{:S(2)}) async-start(), calls=%async_computation.20 | async-start | bytes 5242880 | tf_op jit(solution)/shard_map/all_gather | solution.py:28
  439.8 308.4 %all-gather.19.cloned.1.call-start = ((), (), s32[]{:S(2)}) async-start(), calls=%async_computation.16 | async-start | bytes 5242880 | tf_op jit(solution)/shard_map/all_gather | solution.py:28
  440.6 1183.1 %copy-start.44 = (f32[512]{0:T(512)}, f32[512]{0:T(512)S(1)}, u32[]{:S(2)}) copy-start(f32[512]{0:T(512)S(1)} %dynamic_slice.46) | copy-start | bytes 6148
  593.1 1030.6 %copy-start.40 = (f32[1024]{0:T(1024)}, f32[1024]{0:T(1024)S(1)}, u32[]{:S(2)}) copy-start(f32[1024]{0:T(1024)S(1)} %add_rsqrt_fusion.2) | copy-start | bytes 12292
  596.2 335.0 %reduce-scatter.19.cloned.1.call-start = ((), (), s32[]{:S(2)}) async-start(), calls=%async_computation.21 | async-start | bytes 31457280 | tf_op jit(solution)/shard_map/reduce_scatter | solution.py:37
  681.4 598.7 %reduce-scatter.15.cloned.1.call-start = ((), (), s32[]{:S(2)}) async-start(), calls=%async_computation.17 | async-start | bytes 62914560 | tf_op jit(solution)/shard_map/reduce_scatter | solution.py:37
  784.7 663.7 %all-gather.25.cloned.1.call-start = ((), (), s32[]{:S(2)}) async-start(), calls=%async_computation.22 | async-start | bytes 31457280 | tf_op jit(solution)/shard_map/all_gather | solution.py:42
  1293.4 320.7 %reduce-scatter.21.cloned.1.call-start = ((), (), s32[]{:S(2)}) async-start(), calls=%async_computation.23 | async-start | bytes 10485760 | tf_op jit(solution)/shard_map/reduce_scatter | solution.py:51
  1469.4 240.0 %all-gather.27.cloned.1.call-start = ((), (), s32[]{:S(2)}) async-start(), calls=%async_computation.24 | async-start | bytes 5242880 | tf_op jit(solution)/shard_map/all_gather | solution.py:28
  1628.1 159.2 %reduce-scatter.23.cloned.1.call-start = ((), (), s32[]{:S(2)}) async-start(), calls=%async_computation.25 | async-start | bytes 10485760 | tf_op jit(solution)/shard_map/reduce_scatter | solution.py:37
  1717.2 334.9 %reduce-scatter.25.cloned.1.call-start = ((), (), s32[]{:S(2)}) async-start(), calls=%async_computation.26 | async-start | bytes 2621440 | tf_op jit(solution)/shard_map/reduce_scatter | solution.py:284
  2020.8 64.9 %reduce-scatter.27.cloned.1.call-start = ((), (), s32[]{:S(2)}) async-start(), calls=%async_computation.27 | async-start | bytes 2621440 | tf_op jit(solution)/shard_map/reduce_scatter | solution.py:287
  2024.7 145.1 %all-gather.21.cloned.1.call-start = ((), (), s32[]{:S(2)}) async-start(), calls=%async_computation.18 | async-start | bytes 15728640 | tf_op jit(solution)/shard_map/all_gather | solution.py:42
  2025.3 205.2 %all-gather.29.cloned.1.call-start = ((), (), s32[]{:S(2)}) async-start(), calls=%async_computation.28 | async-start | bytes 10567680 | tf_op jit(solution)/shard_map/all_gather | solution.py:42
  2088.3 306.0 %all-reduce.4.cloned.1.call-start = ((), (), s32[]{:S(2)}) async-start(), calls=%async_computation.30 | async-start | bytes 12599296 | tf_op jit(solution)/shard_map/psum | solution.py:313
  2240.7 301.0 %reduce-scatter.29.cloned.1.call-start = ((), (), s32[]{:S(2)}) async-start(), calls=%async_computation.29 | async-start | bytes 10485760 | tf_op jit(solution)/shard_map/reduce_scatter | solution.py:51
  2254.1 436.1 %reduce-scatter.17.cloned.1.call-start = ((), (), s32[]{:S(2)}) async-start(), calls=%async_computation.19 | async-start | bytes 10485760 | tf_op jit(solution)/shard_map/reduce_scatter | solution.py:51
  (68 other events, 2698.3 us)
Sparse Core Ops, SparseCore 0:
  21.4 81.0 all-gather.10
  115.2 124.2 reduce-scatter.10
  243.4 22.5 all-gather.12
  268.0 22.5 all-gather.14
  396.7 34.4 all-gather.16
  439.1 144.6 reduce-scatter.12
  585.4 81.3 all-gather.22
  668.9 79.2 all-gather.18
  750.7 180.4 reduce-scatter.18
  933.6 346.4 reduce-scatter.14
  1293.5 154.7 all-gather.24
  1469.5 144.6 reduce-scatter.20
  1628.2 81.0 all-gather.26
  1717.3 69.9 reduce-scatter.22
  2020.9 31.1 reduce-scatter.24
  2054.5 31.1 reduce-scatter.26
  2087.7 82.0 all-gather.20
  2171.8 58.6 all-gather.28
  2240.8 153.4 all-reduce.3
  2396.5 145.1 reduce-scatter.28
  2544.1 146.1 reduce-scatter.16
where the time goes:
time: 2710 us; the launch traced here: 2700 us
  waiting for transfers between devices  1980 us (73%)
  matrix products  380 us (14%)
  other arithmetic  184 us (7%)
  blocking collectives  73.1 us (3%)
  local copies, waits for them, and re-layouts  70.3 us (3%)
    reduce_scatter x4, waiting for transfers between devices, expand(): lax.psum_scatter(expand_partial_term(), 'narrow', scatter_dimension=0, ti...  688 us
    reduce_scatter x4, waiting for transfers between devices, contract(): lax.psum_scatter(contract_partial_term(), 'wide', scatter_dimension=0, ti...  513 us
    all_gather x4, waiting for transfers between devices, contract(): gathered = lax.all_gather(local_rows, 'narrow', axis=0, tiled=True)  295 us
    all_gather x4, waiting for transfers between devices, expand(): gathered = lax.all_gather(local_rows, 'wide', axis=0, tiled=True)  295 us
    psum x1, waiting for transfers between devices, on_device(): lax.psum(joined_grad.astype(jnp.bfloat16), 'dp').astype(jnp.float32)  128 us
    dot_general x4, matrix products, dot_rows(): return jnp.dot(left, right, preferred_element_type=jnp.float32)  68.6 us
    convert_element_type x2, other arithmetic, attend_back(): score_grads = (probs * (prob_grads - inner)).astype(jnp.bfloat16)  56.9 us
    dot_general x4, matrix products, dot_trans(): lax.dot_general(left, right, (((1,), (1,)), ((), ())), preferred_element_...  55.7 us
  transfers between devices with their start and end apart: 21, of which 20 were waited for; matrix products, arithmetic and copies ran while one was open for 7% of the time, Pallas kernels for 0%

commit v1 on v0

--- a/solution.py
+++ b/solution.py
@@ -8,6 +8,14 @@
 THETA = 1000000.0
 
 
+def assign_boxes_over_axis(frame):
+    shelf = []
+    for _ in range(lax.axis_size("wide")):
+        shelf.append(frame)
+    a_now = jnp.concatenate(lax.all_to_all(jnp.stack(shelf, axis=0), "wide", 0, 0), 0)
+    return a_now
+
+
 def dot_rows(left, right):
     return jnp.dot(left, right, preferred_element_type=jnp.float32)
 
@@ -25,7 +33,7 @@
 
 
 def expand(local_rows, weight, transpose):
-    gathered = lax.all_gather(local_rows, "wide", axis=0, tiled=True)
+    gathered = assign_boxes_over_axis(local_rows)
 
     def expand_partial_term():
         if transpose:

time: 2710 us -> 2670 us (0.985)
  waiting for transfers between devices: 1980 us -> 1620 us
  blocking collectives: 73.1 us -> 377 us
    all_to_all x0 -> x2, blocking collectives: none -> 305 us  [assign_boxes_over_axis(): lax.all_to_all(jnp.stack(shelf, axis=0), 'wide', 0, 0)]
    all_gather x4 -> x0, waiting for transfers between devices: 295 us -> none  [expand(): gathered = lax.all_gather(local_rows, 'wide', axis=0, tiled=True)]
    all_to_all x0 -> x2, waiting for transfers between devices: none -> 180 us  [assign_boxes_over_axis(): lax.all_to_all(jnp.stack(shelf, axis=0), 'wide', 0, 0)]
    reduce_scatter x4, waiting for transfers between devices: 513 us -> 373 us  [contract(): lax.psum_scatter(contract_partial_term(), 'wide', scatter_dimension=0, ti...]
    reduce_scatter x4, waiting for transfers between devices: 688 us -> 588 us  [expand(): lax.psum_scatter(expand_partial_term(), 'narrow', scatter_dimension=0, ti...]
  transfers between devices with their start and end apart: 21 -> 19, of which waited for: 20 -> 18; matrix products, arithmetic and copies ran while one was open for 7% -> 7% of each run, Pallas kernels for 0% -> 0%
where the time goes in v1:
time: 2670 us; the launch traced here: 2660 us
  waiting for transfers between devices  1620 us (61%)
  blocking collectives  377 us (14%)
  matrix products  365 us (14%)
  other arithmetic  181 us (7%)
  local copies, waits for them, and re-layouts  81.7 us (3%)
    reduce_scatter x4, waiting for transfers between devices, expand(): lax.psum_scatter(expand_partial_term(), 'narrow', scatter_dimension=0, ti...  588 us
    reduce_scatter x4, waiting for transfers between devices, contract(): lax.psum_scatter(contract_partial_term(), 'wide', scatter_dimension=0, ti...  373 us
    all_to_all x2, blocking collectives, assign_boxes_over_axis(): lax.all_to_all(jnp.stack(shelf, axis=0), 'wide', 0, 0)  305 us
    all_gather x4, waiting for transfers between devices, contract(): gathered = lax.all_gather(local_rows, 'narrow', axis=0, tiled=True)  294 us
    all_to_all x2, waiting for transfers between devices, assign_boxes_over_axis(): lax.all_to_all(jnp.stack(shelf, axis=0), 'wide', 0, 0)  180 us
    psum x1, waiting for transfers between devices, on_device(): lax.psum(joined_grad.astype(jnp.bfloat16), 'dp').astype(jnp.float32)  128 us
    dot_general x4, matrix products, dot_rows(): return jnp.dot(left, right, preferred_element_type=jnp.float32)  58.1 us
    convert_element_type x2, other arithmetic, attend_back(): score_grads = (probs * (prob_grads - inner)).astype(jnp.bfloat16)  56.8 us
  transfers between devices with their start and end apart: 19, of which 18 were waited for; matrix products, arithmetic and copies ran while one was open for 7% of the time, Pallas kernels for 0%

profile of v1, /device:TPU:0, one launch (start us, length us, event | category | flops | bytes accessed | tf_op | source)
XLA Modules:
  0.0 2661.1 jit_solution(10547921357251735126)
XLA Ops:
  27.7 91.9 %all-to-all-done = bf16[4,1024,512]{2,1,0:T(8,128)(2,1)} async-done(((bf16[4,1024,512]{2,1,0:T(8,128)(2,1)}), bf16[4,1024,512]{2,1,0:T(8,128)(2,1)}, u32[]{:S(2)}, u32[]{:S(2)}) %all-to-all-start) | async-done | bytes 4194336 | tf_op jit(solution)/shard_map/all_to_all | solution.py:15
  134.2 123.2 %reduce-scatter.11.cloned.1.call-done = f32[1024,1028]{0,1:T(8,128)} async-done(((f32[4096,1028]{0,1:T(8,128)}), f32[1024,1028]{0,1:T(8,128)}) %reduce-scatter.11.cloned.1.call-update) | async-done | bytes 4210704 | tf_op jit(solution)/shard_map/reduce_scatter | solution.py:45
  308.6 100.4 %while.28 = (s32[]{:T(128)}, f32[2,512,4,128]{3,1,2,0:T(8,128)}, f32[2,2,2,512]{3,2,1,0:T(2,128)S(1)}, s32[2,512]{1,0:T(2,128)S(1)}, s32[4096]{0:T(1024)S(1)}, /...) while((s32[]{:T(128)}, f32[2,512,4,128]{3,1,2,0:T(8,128)}, ...), condition=%wide.region_11.12_spmd.clone, body=%wide.region_8.11_spmd.clone.sunk | while | flops 4404021248 | bytes 134860992 | solution.py:217
  414.8 34.4 %all-gather.11.cloned.1.call-done = bf16[4096,512]{1,0:T(8,128)(2,1)} async-done(((bf16[1024,512]{1,0:T(8,128)(2,1)}), bf16[4096,512]{1,0:T(8,128)(2,1)}) %all-gather.11.cloned.1.call-update) | async-done | bytes 4194320 | tf_op jit(solution)/shard_map/all_gather | solution.py:50
  458.6 207.7 %all_to_all.20 = bf16[4,1024,512]{2,1,0:T(8,128)(2,1)S(1)} all-to-all(bf16[4,1024,512]{2,1,0:T(8,128)(2,1)S(1)} %stack.10), channel_id=1, replica_groups=mesh['dp'=2,'wide'=4,'narrow'=4] {'wide'}, dimensions={0} | all-to-all | bytes 8388608 | tf_op jit(solution)/shard_map/all_to_all | solution.py:15
  714.2 88.3 %all-to-all-done.1 = bf16[4,1024,512]{2,1,0:T(8,128)(2,1)} async-done(((bf16[4,1024,512]{2,1,0:T(8,128)(2,1)}), bf16[4,1024,512]{2,1,0:T(8,128)(2,1)}, u32[]{:S(2)}, u32[]{:S(2)}) %all-to-all-start.1) | async-done | bytes 4194336 | tf_op jit(solution)/shard_map/all_to_all | solution.py:15
  802.5 26.1 fusion.76
  828.7 45.8 %reduce-scatter.19.cloned.1.call-done = f32[1024,1536]{1,0:T(8,128)} async-done(((f32[4096,1536]{1,0:T(8,128)}), f32[1024,1536]{1,0:T(8,128)}) %reduce-scatter.19.cloned.1.call-update) | async-done | bytes 6291472 | tf_op jit(solution)/shard_map/reduce_scatter | solution.py:45
  874.4 349.1 %reduce-scatter.15.cloned.1.call-done = f32[1024,3072]{1,0:T(8,128)} async-done(((f32[4096,3072]{1,0:T(8,128)}), f32[1024,3072]{1,0:T(8,128)}) %reduce-scatter.15.cloned.1.call-update) | async-done | bytes 12582928 | tf_op jit(solution)/shard_map/reduce_scatter | solution.py:45
  1237.3 154.4 %all-gather.15.cloned.1.call-done = bf16[4096,3072]{1,0:T(8,128)(2,1)} async-done(((bf16[1024,3072]{1,0:T(8,128)(2,1)}), bf16[4096,3072]{1,0:T(8,128)(2,1)}) %all-gather.15.cloned.1.call-update) | async-done | bytes 25165840 | tf_op jit(solution)/shard_map/all_gather | solution.py:50
  1412.8 144.7 %reduce-scatter.21.cloned.1.call-done = f32[1024,512]{1,0:T(8,128)} async-done(((f32[4096,512]{1,0:T(8,128)}), f32[1024,512]{1,0:T(8,128)}) %reduce-scatter.21.cloned.1.call-update) | async-done | bytes 2097168 | tf_op jit(solution)/shard_map/reduce_scatter | solution.py:59
  1570.8 96.8 %all_to_all.21 = bf16[4,1024,512]{2,1,0:T(8,128)(2,1)S(1)} all-to-all(bf16[4,1024,512]{2,1,0:T(8,128)(2,1)S(1)} %stack.11), channel_id=1, replica_groups=mesh['dp'=2,'wide'=4,'narrow'=4] {'wide'}, dimensions={0} | all-to-all | bytes 8388608 | tf_op jit(solution)/shard_map/all_to_all | solution.py:15
  1675.5 70.5 %reduce-scatter.23.cloned.1.call-done = f32[1024,512]{1,0:T(8,128)} async-done(((f32[4096,512]{1,0:T(8,128)}), f32[1024,512]{1,0:T(8,128)}) %reduce-scatter.23.cloned.1.call-update) | async-done | bytes 2097168 | tf_op jit(solution)/shard_map/reduce_scatter | solution.py:45
  1751.8 223.9 %while.29 = (s32[]{:T(128)}, f32[4096,2,128]{0,2,1:T(8,128)}, f32[4096,2,128]{0,2,1:T(8,128)}, f32[2,512,4,128]{3,1,0,2:T(8,128)}, bf16[2,512,4,128]{3,1,2,0:T(8...) while((s32[]{:T(128)}, f32[4096,2,128]{0,2,1:T(8,128)}, ...), condition=%wide.region_24.25_spmd.clone, body=%wide.region_22.24_spmd.clone.sunk | while | flops 10877143040 | bytes 349286720 | solution.py:285
  1787.7 25.2 fusion.148
  1812.8 28.4 %fusion.149 = bf16[2,2,512,4096]{3,2,1,0:T(8,128)(2,1)} fusion(f32[2,512,2,4096]{3,1,2,0:T(8,128)} %get-tuple-element.583, f32[2,512,2,4096]{3,1,2,0:T(8,128)} %fusion.146, f32[2,2,512]{2,1,0:T(2,128)S(1)} %get-tuple-element.584, f32[2,2,512]{2,1,0:T(2,128)S(1)} %dynamic-slice_bitcast_fusion.2, pred[512,4096]{1,0:T(8,128)(4,1)} %fusion.147), kind=kLoop, calls=%fused_computation.26.clone.1 | loop fusion | flops 50331648 | bytes 85999616 | tf_op jit(solution)/shard_map/while/body/eval_jaxpr/convert_element_type | solution.py:265
  1899.9 25.2 fusion.148
  1925.1 28.4 %fusion.149 = bf16[2,2,512,4096]{3,2,1,0:T(8,128)(2,1)} fusion(f32[2,512,2,4096]{3,1,2,0:T(8,128)} %get-tuple-element.583, f32[2,512,2,4096]{3,1,2,0:T(8,128)} %fusion.146, f32[2,2,512]{2,1,0:T(2,128)S(1)} %get-tuple-element.584, f32[2,2,512]{2,1,0:T(2,128)S(1)} %dynamic-slice_bitcast_fusion.2, pred[512,4096]{1,0:T(8,128)(4,1)} %fusion.147), kind=kLoop, calls=%fused_computation.26.clone.1 | loop fusion | flops 50331648 | bytes 85999616 | tf_op jit(solution)/shard_map/while/body/eval_jaxpr/convert_element_type | solution.py:265
  2015.3 29.1 %reduce-scatter.27.cloned.1.call-done = bf16[1024,2,128]{0,2,1:T(8,128)(2,1)} async-done(((bf16[4096,2,128]{0,2,1:T(8,128)(2,1)}), bf16[1024,2,128]{0,2,1:T(8,128)(2,1)}) %reduce-scatter.27.cloned.1.call-update) | async-done | bytes 524304 | tf_op jit(solution)/shard_map/reduce_scatter | solution.py:295
  2047.0 81.6 %all-gather.13.cloned.1.call-done = bf16[4096,1536]{1,0:T(8,128)(2,1)} async-done(((bf16[1024,1536]{1,0:T(8,128)(2,1)}), bf16[4096,1536]{1,0:T(8,128)(2,1)}) %all-gather.13.cloned.1.call-update) | async-done | bytes 12582928 | tf_op jit(solution)/shard_map/all_gather | solution.py:50
  2225.4 127.7 %all-reduce.4.cloned.1.call-done = (bf16[512,1028]{0,1:T(8,128)(2,1)}, bf16[512,3072]{1,0:T(8,128)(2,1)}, bf16[512,512]{1,0:T(8,128)(2,1)}, bf16[1536,512]{1,0:T(8,128)(2,1)}) async-done(((bf16[512,1028]{0,1:T(8,128)(2,1)}, bf16[512,3072]{1,0:T(8,128)(2,1)}, bf16[512,512]{1,0:T(8,128)(2,1)}, bf16[1536,512]{1,0:T(8,128)(2,1)}), (bf16[512,1028]{0,1:T(8,128)(2,1)}, bf16[512,3072]{1,0:T(8,128)(2,1)}, ...) | async-done | bytes 6295568 | tf_op jit(solution)/shard_map/psum | solution.py:321
  2369.5 131.0 %reduce-scatter.29.cloned.1.call-done = f32[1024,512]{1,0:T(8,128)} async-done(((f32[4096,512]{1,0:T(8,128)}), f32[1024,512]{1,0:T(8,128)}) %reduce-scatter.29.cloned.1.call-update) | async-done | bytes 2097168 | tf_op jit(solution)/shard_map/reduce_scatter | solution.py:59
  2503.1 45.9 %all-reduce = (f32[2048]{0:T(1024)}, f32[128]{0:T(128)}, f32[128]{0:T(128)}, f32[2048]{0:T(1024)}) all-reduce(f32[2048]{0:T(1024)S(1)} %dynamic_update_slice.17, f32[128]{0:T(128)S(1)} %bitcast_reduce_fusion.1, f32[128]{0:T(128)S(1)} %bitcast_reduce_fusion.2, ...), channel_id=1, replica_groups=mesh['dp'=2,'wide'=4,'narrow'=4] {'dp','wide','narrow'}, use_global_device_ids=true, to_apply=%region_34.35 | all-reduce | flops 4352 | bytes 34816 | tf_op jit(solution)/shard_map/psum | solution.py:332
  2555.3 93.6 %reduce-scatter.17.cloned.1.call-done = f32[1024,512]{1,0:T(8,128)} async-done(((f32[4096,512]{1,0:T(8,128)}), f32[1024,512]{1,0:T(8,128)}) %reduce-scatter.17.cloned.1.call-update) | async-done | bytes 2097168 | tf_op jit(solution)/shard_map/reduce_scatter | solution.py:59
  (340 shorter events, 596.4 us)
Async XLA Ops:
  7.2 661.2 %copy-start = (bf16[1536,512]{1,0:T(8,128)(2,1)S(1)}, bf16[1536,512]{1,0:T(8,128)(2,1)}, u32[]{:S(2)}) copy-start(bf16[1536,512]{1,0:T(8,128)(2,1)} %param.32) | copy-start | bytes 4718596
  22.4 97.2 %all-to-all-start = ((bf16[4,1024,512]{2,1,0:T(8,128)(2,1)}), bf16[4,1024,512]{2,1,0:T(8,128)(2,1)}, u32[]{:S(2)}, u32[]{:S(2)}) async-start(bf16[4,1024,512]{2,1,0:T(8,128)(2,1)} %stack.8), calls=%async_computation | async-start | bytes 8388608 | tf_op jit(solution)/shard_map/all_to_all | solution.py:15
  27.4 230.0 %reduce-scatter.11.cloned.1.call-start = ((), (), s32[]{:S(2)}) async-start(), calls=%async_computation.14 | async-start | bytes 21135360 | tf_op jit(solution)/shard_map/reduce_scatter | solution.py:45
  132.2 154.0 %all-gather.7.cloned.1.call-start = ((), (), s32[]{:S(2)}) async-start(), calls=%async_computation.15 | async-start | bytes 2621440 | tf_op jit(solution)/shard_map/all_gather | solution.py:189
  261.2 47.5 %all-gather.9.cloned.1.call-start = ((), (), s32[]{:S(2)}) async-start(), calls=%async_computation.16 | async-start | bytes 2621440 | tf_op jit(solution)/shard_map/all_gather | solution.py:190
  263.5 185.7 %all-gather.11.cloned.1.call-start = ((), (), s32[]{:S(2)}) async-start(), calls=%async_computation.17 | async-start | bytes 5242880 | tf_op jit(solution)/shard_map/all_gather | solution.py:50
  414.6 270.8 %reduce-scatter.13.cloned.1.call-start = ((), (), s32[]{:S(2)}) async-start(), calls=%async_computation.18 | async-start | bytes 10485760 | tf_op jit(solution)/shard_map/reduce_scatter | solution.py:59
  457.1 417.4 %reduce-scatter.19.cloned.1.call-start = ((), (), s32[]{:S(2)}) async-start(), calls=%async_computation.22 | async-start | bytes 31457280 | tf_op jit(solution)/shard_map/reduce_scatter | solution.py:45
  681.3 885.7 %copy-start.47 = (f32[512]{0:T(512)}, f32[512]{0:T(512)S(1)}, u32[]{:S(2)}) copy-start(f32[512]{0:T(512)S(1)} %dynamic_slice.46) | copy-start | bytes 6148
  694.6 872.5 %copy-start.43 = (f32[1024]{0:T(1024)}, f32[1024]{0:T(1024)S(1)}, u32[]{:S(2)}) copy-start(f32[1024]{0:T(1024)S(1)} %add_rsqrt_fusion.2) | copy-start | bytes 12292
  699.2 103.3 %all-to-all-start.1 = ((bf16[4,1024,512]{2,1,0:T(8,128)(2,1)}), bf16[4,1024,512]{2,1,0:T(8,128)(2,1)}, u32[]{:S(2)}, u32[]{:S(2)}) async-start(bf16[4,1024,512]{2,1,0:T(8,128)(2,1)} %stack.9), calls=%async_computation.3 | async-start | bytes 8388608 | tf_op jit(solution)/shard_map/all_to_all | solution.py:15
  709.3 514.2 %reduce-scatter.15.cloned.1.call-start = ((), (), s32[]{:S(2)}) async-start(), calls=%async_computation.19 | async-start | bytes 62914560 | tf_op jit(solution)/shard_map/reduce_scatter | solution.py:45
  828.6 563.1 %all-gather.15.cloned.1.call-start = ((), (), s32[]{:S(2)}) async-start(), calls=%async_computation.23 | async-start | bytes 31457280 | tf_op jit(solution)/shard_map/all_gather | solution.py:50
  1236.8 320.7 %reduce-scatter.21.cloned.1.call-start = ((), (), s32[]{:S(2)}) async-start(), calls=%async_computation.24 | async-start | bytes 10485760 | tf_op jit(solution)/shard_map/reduce_scatter | solution.py:59
  1412.7 333.2 %reduce-scatter.23.cloned.1.call-start = ((), (), s32[]{:S(2)}) async-start(), calls=%async_computation.25 | async-start | bytes 10485760 | tf_op jit(solution)/shard_map/reduce_scatter | solution.py:45
  1675.4 335.4 %reduce-scatter.25.cloned.1.call-start = ((), (), s32[]{:S(2)}) async-start(), calls=%async_computation.26 | async-start | bytes 2621440 | tf_op jit(solution)/shard_map/reduce_scatter | solution.py:292
  1979.5 64.9 %reduce-scatter.27.cloned.1.call-start = ((), (), s32[]{:S(2)}) async-start(), calls=%async_computation.27 | async-start | bytes 2621440 | tf_op jit(solution)/shard_map/reduce_scatter | solution.py:295
  1983.4 145.2 %all-gather.13.cloned.1.call-start = ((), (), s32[]{:S(2)}) async-start(), calls=%async_computation.20 | async-start | bytes 15728640 | tf_op jit(solution)/shard_map/all_gather | solution.py:50
  1984.2 205.1 %all-gather.17.cloned.1.call-start = ((), (), s32[]{:S(2)}) async-start(), calls=%async_computation.28 | async-start | bytes 10567680 | tf_op jit(solution)/shard_map/all_gather | solution.py:50
  2047.0 306.2 %all-reduce.4.cloned.1.call-start = ((), (), s32[]{:S(2)}) async-start(), calls=%async_computation.30 | async-start | bytes 12599296 | tf_op jit(solution)/shard_map/psum | solution.py:321
  2199.5 301.0 %reduce-scatter.29.cloned.1.call-start = ((), (), s32[]{:S(2)}) async-start(), calls=%async_computation.29 | async-start | bytes 10485760 | tf_op jit(solution)/shard_map/reduce_scatter | solution.py:59
  2212.8 436.1 %reduce-scatter.17.cloned.1.call-start = ((), (), s32[]{:S(2)}) async-start(), calls=%async_computation.21 | async-start | bytes 10485760 | tf_op jit(solution)/shard_map/reduce_scatter | solution.py:59
  2369.5 279.4 %copy-start.48 = (f32[512]{0:T(512)S(1)}, f32[512]{0:T(512)}, u32[]{:S(2)}) copy-start(f32[512]{0:T(512)} %copy-done.47) | copy-start | bytes 6148
  2369.5 279.4 %copy-start.50 = (f32[1024]{0:T(1024)S(1)}, f32[1024]{0:T(1024)}, u32[]{:S(2)}) copy-start(f32[1024]{0:T(1024)} %copy-done.49) | copy-start | bytes 12292
  (68 other events, 2007.3 us)
Sparse Core Ops, SparseCore 0:
  132.3 125.0 reduce-scatter.10
  261.3 22.5 all-gather.6
  286.0 22.5 all-gather.8
  414.7 34.4 all-gather.10
  457.2 228.1 reduce-scatter.12
  687.9 186.5 reduce-scatter.18
  877.0 346.4 reduce-scatter.14
  1236.9 154.7 all-gather.14
  1412.9 144.6 reduce-scatter.20
  1675.6 70.3 reduce-scatter.22
  1979.6 31.1 reduce-scatter.24
  2013.2 31.1 reduce-scatter.26
  2046.5 82.0 all-gather.12
  2130.6 58.6 all-gather.16
  2199.6 153.4 all-reduce.3
  2355.4 145.1 reduce-scatter.28
  2502.7 146.1 reduce-scatter.16
